TPU v7x, 32 devices: a whole 2x2x4 slice. The times are simulated.
32 devices in a mesh: sweep: 2 (over x), recv: 16 (over z, y, core).
Axes of the slice: x: 2, y: 2, z: 4, core: 2. Of those that a mesh axis runs over, the one named last changes fastest.
Arguments:
- records: bfloat16 [16, 1024, 4096], P('sweep', 'recv'), may hold values from -6 to 6
- pilots: bfloat16 [16, 3968], replicated, may hold values from -0.09375 to 0.09375
- hadamard: int32 [16, 16], replicated, may hold values from -1 to 1, as said below
- code_vibrator: int32 [16], replicated, may hold values from 0 to 15, each once
- owner_map: int32 [1024], P('recv'), may hold values from 0 to 15
- live_mask: int32 [1024], P('recv'), may hold values 0 or 1
- filters: bfloat16 [16, 128, 128], P('sweep'), may hold values from -0.5 to 0.5
- targets: bfloat16 [16, 1024, 128], P('sweep', 'recv'), may hold values from -6 to 6
Outputs:
- responses: float32 [16, 1024, 128], P('sweep', 'recv')
- gradient: float32 [16, 128, 128], P('sweep', 'recv')
Inputs may be any that keep to these rules, and one draw needn't show every extreme that they name: hadamard transposed times hadamard is 16 times the identity. `code_vibrator`: every vibrator belongs to exactly one code.
All inputs are finite; a program needn't handle non-finite values. No bound on the sum of `live_mask` on one device may be relied on, other than what follows from the above.
Results may differ from a plain program's by a relative error of at most 0.0085.
Values may be sent and summed in bfloat16 or wider, within the bound.
No kernel may reach another device: no remote copies, remote signals or barrier semaphores. Data moves between devices by JAX's collectives and lax.ppermute only.
A program may use at most 64 MiB of HBM per device.

v0:
```python
import math
import jax
import jax.numpy as jnp
from jax import lax
from jax.sharding import PartitionSpec as P


def toeplitz(sweep_pilot, samples, lagcount):
    padding = jnp.zeros((samples + 1 - sweep_pilot.shape[0],), sweep_pilot.dtype)
    extended = jnp.concatenate([sweep_pilot, padding])
    return jnp.tile(extended, lagcount)[: lagcount * samples].reshape(lagcount, samples)


def correlate_split(combined, sweep_pilot, samples, lagcount):
    upper = combined.astype(jnp.bfloat16)
    lower = (combined - upper.astype(jnp.float32)).astype(jnp.bfloat16)
    paired = jnp.concatenate([upper, lower], axis=0)
    toe_rows = toeplitz(sweep_pilot, samples, lagcount)
    lagged = lax.dot_general(
        paired, toe_rows, (((1,), (1,)), ((), ())), preferred_element_type=jnp.float32
    )
    half = combined.shape[0]
    return lagged[:half] + lagged[half:]


def local(records, pilots, hadamard, code_vibrator, owner_map, live_mask, filters, targets):
    sweeps = lax.axis_size("sweep")
    codes = hadamard.shape[1]
    held_sweeps = records.shape[0]
    channels = records.shape[1]
    samples = records.shape[2]
    lagcount = filters.shape[1]
    owned_codes = filters.shape[0]
    first_code = lax.axis_index("sweep") * owned_codes
    code_norm = 1.0 / math.sqrt(codes)
    onehot = (code_vibrator[:, None] == jnp.arange(codes, dtype=jnp.int32)[None, :]).astype(
        jnp.bfloat16
    )
    code_pilot = jnp.dot(onehot, pilots, preferred_element_type=jnp.float32).astype(jnp.bfloat16)
    blocks = records.reshape(held_sweeps, sweeps, channels // sweeps, samples)
    gathered = lax.all_to_all(blocks, "sweep", split_axis=1, concat_axis=0, tiled=True)
    gathered = gathered.reshape(codes, channels // sweeps, samples)
    decoded_raw = jnp.einsum(
        "sc,srt->crt", hadamard.astype(jnp.bfloat16), gathered, preferred_element_type=jnp.float32
    )

    def column(operands):
        decoded_line, sweep_pilot = operands
        return code_norm * correlate_split(decoded_line, sweep_pilot, samples, lagcount)

    all_codes = lax.map(column, (decoded_raw, code_pilot)).astype(jnp.bfloat16)
    decoded = lax.all_to_all(all_codes, "sweep", split_axis=0, concat_axis=1, tiled=True)
    col_vibs = lax.dynamic_slice_in_dim(code_vibrator, first_code, owned_codes, 0)
    responses = jnp.einsum("crl,clm->crm", decoded, filters, preferred_element_type=jnp.float32)
    owned = (owner_map[None, :] == col_vibs[:, None]).astype(jnp.float32)
    weight = live_mask.astype(jnp.float32)[None, :] * (0.25 + owned)
    residual = (weight[:, :, None] * (responses - targets.astype(jnp.float32))).astype(jnp.bfloat16)
    factor = 1.0 / math.sqrt(channels * lax.axis_size("recv"))
    local_grad = (
        jnp.einsum("crl,crm->clm", decoded, residual, preferred_element_type=jnp.float32) * factor
    )
    summed = lax.psum(local_grad, "recv")
    share_rows = lagcount // lax.axis_size("recv")
    gradient = lax.dynamic_slice_in_dim(summed, lax.axis_index("recv") * share_rows, share_rows, 1)
    return (responses, gradient)


def solution(mesh):
    in_specs = (
        P("sweep", "recv", None),
        P(),
        P(),
        P(),
        P("recv"),
        P("recv"),
        P("sweep", None, None),
        P("sweep", "recv", None),
    )
    out_specs = (P("sweep", "recv", None), P("sweep", "recv", None))
    return jax.shard_map(local, mesh=mesh, in_specs=in_specs, out_specs=out_specs, check_vma=False)
```

profile of v0, /device:TPU:0, one launch (start us, length us, event | category | flops | bytes accessed | tf_op | source)
XLA Modules:
  0.0 284.5 jit_solution(12930026134246366207)
XLA Ops:
  7.2 6.5 %copy.18 = bf16[8,64,4096]{2,0,1:T(8,128)(2,1)} copy(bf16[8,64,4096]{2,1,0:T(8,128)(2,1)} %param.10) | data formatting | bytes 8388608 | tf_op args[0]
  13.7 5.8 %all-to-all-start = ((bf16[8,2,32,4096]{3,0,2,1:T(8,128)(2,1)}), bf16[8,2,32,4096]{3,0,2,1:T(8,128)(2,1)}, u32[]{:S(2)}, u32[]{:S(2)}) async-start(bf16[8,2,32,4096]{3,0,2,1:T(8,128)(2,1)} %bitcast.43), calls=%async_computation | async-start | bytes 8388608 | tf_op jit(solution)/shard_map/all_to_all | solution.py:41
  19.8 48.5 %all-to-all-done = bf16[8,2,32,4096]{3,0,2,1:T(8,128)(2,1)} async-done(((bf16[8,2,32,4096]{3,0,2,1:T(8,128)(2,1)}), bf16[8,2,32,4096]{3,0,2,1:T(8,128)(2,1)}, u32[]{:S(2)}, u32[]{:S(2)}) %all-to-all-start) | async-done | bytes 4194336 | tf_op jit(solution)/shard_map/all_to_all | solution.py:41
  68.3 6.7 %fusion.9 = f32[16,32,4096]{2,0,1:T(8,128)} fusion(s32[16,16]{1,0:T(8,128)S(1)} %copy-done.4, bf16[8,2,32,4096]{3,0,2,1:T(8,128)(2,1)} %all-to-all-done), kind=kOutput, calls=%fused_computation.15 | convolution fusion | flops 67109120 | bytes 12583936 | tf_op jit(solution)/shard_map/sc,srt->crt/dot_general | solution.py:43
  75.0 100.5 %while.10 = (s32[]{:T(128)}, bf16[16,32,128]{2,1,0:T(8,128)(2,1)}, f32[16,32,4096]{2,0,1:T(8,128)}, bf16[16,3968]{1,0:T(8,128)(2,1)S(1)}, s32[]{:T(128)}, /*index=5*/bf16[]{:T(256)}) while((s32[]{:T(128)}, bf16[16,32,128]{2,1,0:T(8,128)(2,1)}, f32[16,32,4096]{2,0,1:T(8,128)}, bf16[16,3968]{1,0:T(8,128)(2,1)S(1)}, s32[]{:T(128)}, ...), condition=%wide.region_1.2_spmd, body=%wide.region_0.1_spmd.sunk | while | flops 68689920 | bytes 11657811 | solution.py:51
  75.0 2.7 constant_dynamic-slice_fusion.3
  78.5 1.2 tile.12
  79.7 0.5 reshape.62
  80.7 0.6 fusion.30
  81.3 2.7 constant_dynamic-slice_fusion.3
  84.8 1.2 tile.12
  87.0 0.6 fusion.30
  87.6 2.7 constant_dynamic-slice_fusion.3
  91.1 1.2 tile.12
  93.3 0.6 fusion.30
  93.9 2.7 constant_dynamic-slice_fusion.3
  97.3 1.2 tile.12
  99.6 0.6 fusion.30
  100.2 2.7 constant_dynamic-slice_fusion.3
  103.6 1.2 tile.12
  104.8 0.5 reshape.62
  105.8 0.6 fusion.30
  106.4 2.7 constant_dynamic-slice_fusion.3
  109.9 1.2 tile.12
  112.1 0.6 fusion.30
  112.7 2.7 constant_dynamic-slice_fusion.3
  116.2 1.2 tile.12
  118.4 0.6 fusion.30
  119.0 2.7 constant_dynamic-slice_fusion.3
  122.4 1.2 tile.12
  124.7 0.6 fusion.30
  125.3 2.7 constant_dynamic-slice_fusion.3
  128.7 1.2 tile.12
  130.9 0.6 fusion.30
  131.6 2.7 constant_dynamic-slice_fusion.3
  135.0 1.2 tile.12
  136.2 0.5 reshape.62
  137.2 0.6 fusion.30
  137.8 2.7 constant_dynamic-slice_fusion.3
  141.3 1.2 tile.12
  143.5 0.6 fusion.30
  144.1 2.7 constant_dynamic-slice_fusion.3
  147.6 1.2 tile.12
  149.8 0.6 fusion.30
  150.4 2.7 constant_dynamic-slice_fusion.3
  153.8 1.2 tile.12
  155.1 0.5 reshape.62
  156.1 0.6 fusion.30
  156.7 2.7 constant_dynamic-slice_fusion.3
  160.1 1.2 tile.12
  161.3 0.5 reshape.62
  162.3 0.6 fusion.30
  162.9 2.7 constant_dynamic-slice_fusion.3
  166.4 1.2 tile.12
  168.6 0.6 fusion.30
  169.2 2.7 constant_dynamic-slice_fusion.3
  172.7 1.2 tile.12
  173.9 0.5 reshape.62
  174.9 0.6 fusion.30
  175.5 3.4 %all-to-all-start.1 = ((bf16[16,32,128]{2,1,0:T(8,128)(2,1)}), bf16[16,32,128]{2,1,0:T(8,128)(2,1)S(1)}, u32[]{:S(2)}, u32[]{:S(2)}) async-start(bf16[16,32,128]{2,1,0:T(8,128)(2,1)} %get-tuple-element.24), calls=%async_computation.1 | async-start | bytes 262144 | tf_op jit(solution)/shard_map/all_to_all | solution.py:52
  179.0 4.3 %all-to-all-done.1 = bf16[16,32,128]{2,1,0:T(8,128)(2,1)S(1)} async-done(((bf16[16,32,128]{2,1,0:T(8,128)(2,1)}), bf16[16,32,128]{2,1,0:T(8,128)(2,1)S(1)}, u32[]{:S(2)}, u32[]{:S(2)}) %all-to-all-start.1) | async-done | bytes 131104 | tf_op jit(solution)/shard_map/all_to_all | solution.py:52
  183.6 1.2 convolution_multiply_fusion
  184.8 91.5 %all-reduce.3.cloned.1.call-done = f32[8,128,128]{2,1,0:T(8,128)} async-done(((f32[8,128,128]{2,1,0:T(8,128)}), f32[8,128,128]{2,1,0:T(8,128)}) %all-reduce.3.cloned.1.call-update) | async-done | bytes 524304 | tf_op jit(solution)/shard_map/psum | solution.py:62
  276.3 1.4 constant_dynamic-slice_fusion.1
  (147 shorter events, 26.2 us)
Async XLA Ops:
  7.2 176.2 %copy-start = (bf16[8,128,128]{2,1,0:T(8,128)(2,1)S(1)}, bf16[8,128,128]{2,1,0:T(8,128)(2,1)}, u32[]{:S(2)}) copy-start(bf16[8,128,128]{2,1,0:T(8,128)(2,1)} %param.16) | copy-start | bytes 786436
  13.7 5.8 %copy-start.7 = (s32[64]{0:T(128)S(1)}, s32[64]{0:T(128)}, u32[]{:S(2)}) copy-start(s32[64]{0:T(128)} %param.15) | copy-start | bytes 772
  13.7 5.8 %copy-start.5 = (s32[16]{0:T(128)S(1)}, s32[16]{0:T(128)}, u32[]{:S(2)}) copy-start(s32[16]{0:T(128)} %param.13) | copy-start | bytes 196
  13.7 5.9 %copy-start.3 = (bf16[16,3968]{1,0:T(8,128)(2,1)S(1)}, bf16[16,3968]{1,0:T(8,128)(2,1)}, u32[]{:S(2)}) copy-start(bf16[16,3968]{1,0:T(8,128)(2,1)} %param.11) | copy-start | bytes 380932
  13.7 54.7 %copy-start.4 = (s32[16,16]{1,0:T(8,128)S(1)}, s32[16,16]{1,0:T(8,128)}, u32[]{:S(2)}) copy-start(s32[16,16]{1,0:T(8,128)} %param.12) | copy-start | bytes 3076
  13.7 54.6 %all-to-all-start = ((bf16[8,2,32,4096]{3,0,2,1:T(8,128)(2,1)}), bf16[8,2,32,4096]{3,0,2,1:T(8,128)(2,1)}, u32[]{:S(2)}, u32[]{:S(2)}) async-start(bf16[8,2,32,4096]{3,0,2,1:T(8,128)(2,1)} %bitcast.43), calls=%async_computation | async-start | bytes 8388608 | tf_op jit(solution)/shard_map/all_to_all | solution.py:41
  75.0 103.9 %copy-start.6 = (s32[64]{0:T(128)S(1)}, s32[64]{0:T(128)}, u32[]{:S(2)}) copy-start(s32[64]{0:T(128)} %param.14) | copy-start | bytes 772
  75.0 108.5 %copy-start.2 = (bf16[8,64,128]{2,1,0:T(8,128)(2,1)S(1)}, bf16[8,64,128]{2,1,0:T(8,128)(2,1)}, u32[]{:S(2)}) copy-start(bf16[8,64,128]{2,1,0:T(8,128)(2,1)} %param.17) | copy-start | bytes 393220
  175.5 7.8 %all-to-all-start.1 = ((bf16[16,32,128]{2,1,0:T(8,128)(2,1)}), bf16[16,32,128]{2,1,0:T(8,128)(2,1)S(1)}, u32[]{:S(2)}, u32[]{:S(2)}) async-start(bf16[16,32,128]{2,1,0:T(8,128)(2,1)} %get-tuple-element.24), calls=%async_computation.1 | async-start | bytes 262144 | tf_op jit(solution)/shard_map/all_to_all | solution.py:52
  178.9 97.4 %all-reduce.3.cloned.1.call-start = ((), (), s32[]{:S(2)}) async-start(), calls=%async_computation.2 | async-start | bytes 1048576 | tf_op jit(solution)/shard_map/psum | solution.py:62
  183.6 94.1 %copy-start.1 = (f32[8,64,128]{2,1,0:T(8,128)}, f32[8,64,128]{2,1,0:T(8,128)S(1)}, u32[]{:S(2)}) copy-start(f32[8,64,128]{2,1,0:T(8,128)S(1)} %fusion.16) | copy-start | bytes 786436
Sparse Core Ops, SparseCore 0:
  184.9 91.3 all-reduce.2
where the time goes:
time: 285 us; the launch traced here: 284 us
  waiting for transfers between devices  144 us (51%)
  local copies, waits for them, and re-layouts  85.3 us (30%)
  matrix products  15.9 us (6%)
  other arithmetic  14.5 us (5%)
  between operations  14.1 us (5%)
  starting transfers between devices  9.19 us (3%)
    psum x1, waiting for transfers between devices, local(): summed = lax.psum(local_grad, 'recv')  91.5 us
    dynamic_slice x48, local copies, waits for them, and re-layouts, local(): all_codes = lax.map(column, (decoded_raw, code_pilot)).astype(jnp.bfloat16)  48.6 us
    all_to_all x1, waiting for transfers between devices, local(): lax.all_to_all(blocks, 'sweep', split_axis=1, concat_axis=0, tiled=True)  48.5 us
    another operation x32, local copies, waits for them, and re-layouts, toeplitz(): jnp.tile(extended, lagcount)[:lagcount * samples].reshape(lagcount, samples)  19.6 us
    dynamic_update_slice x16, other arithmetic, local(): all_codes = lax.map(column, (decoded_raw, code_pilot)).astype(jnp.bfloat16)  9.76 us
    reshape x16, local copies, waits for them, and re-layouts, toeplitz(): jnp.tile(extended, lagcount)[:lagcount * samples].reshape(lagcount, samples)  7.9 us
    dot_general x16, matrix products, correlate_split(): lax.dot_general(paired, toe_rows, (((1,), (1,)), ((), ())), preferred_ele...  7.67 us
    dot_general x1, matrix products, local(): jnp.einsum('sc,srt->crt', hadamard.astype(jnp.bfloat16), gathered, prefer...  6.7 us
  transfers between devices with their start and end apart: 3, of which 3 were waited for; matrix products, arithmetic and copies ran while one was open for 0% of the time, Pallas kernels for 0%

commit v1 on v0

--- a/solution.py
+++ b/solution.py
@@ -59,7 +59,8 @@
     local_grad = (
         jnp.einsum("crl,crm->clm", decoded, residual, preferred_element_type=jnp.float32) * factor
     )
-    summed = lax.psum(local_grad, "recv")
+    parts = lax.all_gather(local_grad, "recv")
+    summed = jnp.sum(parts, axis=0)
     share_rows = lagcount // lax.axis_size("recv")
     gradient = lax.dynamic_slice_in_dim(summed, lax.axis_index("recv") * share_rows, share_rows, 1)
     return (responses, gradient)

time: 285 us -> 272 us (0.954)
  waiting for transfers between devices: 144 us -> 128 us
  other arithmetic: 14.5 us -> 18.5 us
    psum x1 -> x0, waiting for transfers between devices: 91.5 us -> none  [local(): summed = lax.psum(local_grad, 'recv')]
    all_gather x0 -> x1, waiting for transfers between devices: none -> 75 us  [local(): parts = lax.all_gather(local_grad, 'recv')]
    reduce_sum x0 -> x1, other arithmetic: none -> 3.94 us  [local(): summed = jnp.sum(parts, axis=0)]
where the time goes in v1:
time: 272 us; the launch traced here: 271 us
  waiting for transfers between devices  128 us (47%)
  local copies, waits for them, and re-layouts  84.3 us (31%)
  other arithmetic  18.5 us (7%)
  matrix products  16.4 us (6%)
  between operations  14.2 us (5%)
  starting transfers between devices  9.19 us (3%)
    all_gather x1, waiting for transfers between devices, local(): parts = lax.all_gather(local_grad, 'recv')  75 us
    dynamic_slice x48, local copies, waits for them, and re-layouts, local(): all_codes = lax.map(column, (decoded_raw, code_pilot)).astype(jnp.bfloat16)  48.6 us
    all_to_all x1, waiting for transfers between devices, local(): lax.all_to_all(blocks, 'sweep', split_axis=1, concat_axis=0, tiled=True)  48.5 us
    another operation x32, local copies, waits for them, and re-layouts, toeplitz(): jnp.tile(extended, lagcount)[:lagcount * samples].reshape(lagcount, samples)  19.3 us
    dynamic_update_slice x16, other arithmetic, local(): all_codes = lax.map(column, (decoded_raw, code_pilot)).astype(jnp.bfloat16)  9.76 us
    dot_general x16, matrix products, correlate_split(): lax.dot_general(paired, toe_rows, (((1,), (1,)), ((), ())), preferred_ele...  8.02 us
    reshape x16, local copies, waits for them, and re-layouts, toeplitz(): jnp.tile(extended, lagcount)[:lagcount * samples].reshape(lagcount, samples)  7.9 us
    dot_general x1, matrix products, local(): jnp.einsum('sc,srt->crt', hadamard.astype(jnp.bfloat16), gathered, prefer...  6.7 us
  transfers between devices with their start and end apart: 3, of which 3 were waited for; matrix products, arithmetic and copies ran while one was open for 0% of the time, Pallas kernels for 0%

profile of v1, /device:TPU:0, one launch (start us, length us, event | category | flops | bytes accessed | tf_op | source)
XLA Modules:
  0.0 271.3 jit_solution(3084708277067928714)
XLA Ops:
  7.2 6.5 %copy.18 = bf16[8,64,4096]{2,0,1:T(8,128)(2,1)} copy(bf16[8,64,4096]{2,1,0:T(8,128)(2,1)} %param.10) | data formatting | bytes 8388608 | tf_op args[0]
  13.7 5.8 %all-to-all-start = ((bf16[8,2,32,4096]{3,0,2,1:T(8,128)(2,1)}), bf16[8,2,32,4096]{3,0,2,1:T(8,128)(2,1)}, u32[]{:S(2)}, u32[]{:S(2)}) async-start(bf16[8,2,32,4096]{3,0,2,1:T(8,128)(2,1)} %bitcast.44), calls=%async_computation | async-start | bytes 8388608 | tf_op jit(solution)/shard_map/all_to_all | solution.py:41
  19.8 48.5 %all-to-all-done = bf16[8,2,32,4096]{3,0,2,1:T(8,128)(2,1)} async-done(((bf16[8,2,32,4096]{3,0,2,1:T(8,128)(2,1)}), bf16[8,2,32,4096]{3,0,2,1:T(8,128)(2,1)}, u32[]{:S(2)}, u32[]{:S(2)}) %all-to-all-start) | async-done | bytes 4194336 | tf_op jit(solution)/shard_map/all_to_all | solution.py:41
  68.3 6.7 %fusion.9 = f32[16,32,4096]{2,0,1:T(8,128)} fusion(s32[16,16]{1,0:T(8,128)S(1)} %copy-done.4, bf16[8,2,32,4096]{3,0,2,1:T(8,128)(2,1)} %all-to-all-done), kind=kOutput, calls=%fused_computation.15 | convolution fusion | flops 67109120 | bytes 12583936 | tf_op jit(solution)/shard_map/sc,srt->crt/dot_general | solution.py:43
  75.0 100.5 %while.10 = (s32[]{:T(128)}, bf16[16,32,128]{2,1,0:T(8,128)(2,1)}, f32[16,32,4096]{2,0,1:T(8,128)}, bf16[16,3968]{1,0:T(8,128)(2,1)S(1)}, s32[]{:T(128)}, /*index=5*/bf16[]{:T(256)}) while((s32[]{:T(128)}, bf16[16,32,128]{2,1,0:T(8,128)(2,1)}, f32[16,32,4096]{2,0,1:T(8,128)}, bf16[16,3968]{1,0:T(8,128)(2,1)S(1)}, s32[]{:T(128)}, ...), condition=%wide.region_1.2_spmd, body=%wide.region_0.1_spmd.sunk | while | flops 68689920 | bytes 11657811 | solution.py:51
  75.0 2.7 constant_dynamic-slice_fusion.3
  78.5 1.1 tile.12
  80.2 0.5 fusion.29
  80.7 0.6 fusion.30
  81.3 2.7 constant_dynamic-slice_fusion.3
  84.8 1.1 tile.12
  87.0 0.6 fusion.30
  87.6 2.7 constant_dynamic-slice_fusion.3
  91.1 1.1 tile.12
  93.3 0.6 fusion.30
  93.9 2.7 constant_dynamic-slice_fusion.3
  97.3 1.1 tile.12
  99.1 0.5 fusion.29
  99.6 0.6 fusion.30
  100.2 2.7 constant_dynamic-slice_fusion.3
  103.6 1.1 tile.12
  105.3 0.5 fusion.29
  105.8 0.6 fusion.30
  106.5 2.7 constant_dynamic-slice_fusion.3
  109.9 1.1 tile.12
  112.1 0.6 fusion.30
  112.7 2.7 constant_dynamic-slice_fusion.3
  116.2 1.1 tile.12
  118.4 0.6 fusion.30
  119.0 2.7 constant_dynamic-slice_fusion.3
  122.5 1.1 tile.12
  124.7 0.6 fusion.30
  125.3 2.7 constant_dynamic-slice_fusion.3
  128.7 1.1 tile.12
  130.5 0.5 fusion.29
  131.0 0.6 fusion.30
  131.6 2.7 constant_dynamic-slice_fusion.3
  135.0 1.1 tile.12
  137.2 0.6 fusion.30
  137.9 2.7 constant_dynamic-slice_fusion.3
  141.3 1.1 tile.12
  143.5 0.6 fusion.30
  144.1 2.7 constant_dynamic-slice_fusion.3
  147.6 1.1 tile.12
  149.8 0.6 fusion.30
  150.4 2.7 constant_dynamic-slice_fusion.3
  153.9 1.1 tile.12
  155.6 0.5 fusion.29
  156.1 0.6 fusion.30
  156.7 2.7 constant_dynamic-slice_fusion.3
  160.1 1.1 tile.12
  162.4 0.6 fusion.30
  163.0 2.7 constant_dynamic-slice_fusion.3
  166.4 1.1 tile.12
  168.6 0.6 fusion.30
  169.3 2.7 constant_dynamic-slice_fusion.3
  172.7 1.1 tile.12
  174.9 0.6 fusion.30
  175.5 3.4 %all-to-all-start.1 = ((bf16[16,32,128]{2,1,0:T(8,128)(2,1)}), bf16[16,32,128]{2,1,0:T(8,128)(2,1)S(1)}, u32[]{:S(2)}, u32[]{:S(2)}) async-start(bf16[16,32,128]{2,1,0:T(8,128)(2,1)} %get-tuple-element.24), calls=%async_computation.1 | async-start | bytes 262144 | tf_op jit(solution)/shard_map/all_to_all | solution.py:52
  179.1 4.3 %all-to-all-done.1 = bf16[16,32,128]{2,1,0:T(8,128)(2,1)S(1)} async-done(((bf16[16,32,128]{2,1,0:T(8,128)(2,1)}), bf16[16,32,128]{2,1,0:T(8,128)(2,1)S(1)}, u32[]{:S(2)}, u32[]{:S(2)}) %all-to-all-start.1) | async-done | bytes 131104 | tf_op jit(solution)/shard_map/all_to_all | solution.py:52
  183.6 1.2 convolution_multiply_fusion
  184.9 75.0 %all-gather.3.cloned.1.call-done = f32[128,128,128]{2,1,0:T(8,128)} async-done(((f32[8,128,128]{2,1,0:T(8,128)}), f32[128,128,128]{2,1,0:T(8,128)}) %all-gather.3.cloned.1.call-update) | async-done | bytes 8388624 | tf_op jit(solution)/shard_map/all_gather | solution.py:62
  259.9 3.9 %reduce_sum.9 = f32[8,128,128]{2,1,0:T(8,128)S(1)} reduce(f32[16,8,128,128]{3,2,1,0:T(8,128)} %bitcast.45, f32[]{:T(128)} %constant.12.clone.1), dimensions={0}, to_apply=%region_2.3 | reduce | flops 1966080 | bytes 8912900 | tf_op jit(solution)/shard_map/reduce_sum | solution.py:63
  263.9 0.6 constant_dynamic-slice_fusion.1
  (148 shorter events, 27.0 us)
Async XLA Ops:
  7.2 176.2 %copy-start = (bf16[8,128,128]{2,1,0:T(8,128)(2,1)S(1)}, bf16[8,128,128]{2,1,0:T(8,128)(2,1)}, u32[]{:S(2)}) copy-start(bf16[8,128,128]{2,1,0:T(8,128)(2,1)} %param.16) | copy-start | bytes 786436
  13.7 5.8 %copy-start.7 = (s32[64]{0:T(128)S(1)}, s32[64]{0:T(128)}, u32[]{:S(2)}) copy-start(s32[64]{0:T(128)} %param.15) | copy-start | bytes 772
  13.7 5.8 %copy-start.5 = (s32[16]{0:T(128)S(1)}, s32[16]{0:T(128)}, u32[]{:S(2)}) copy-start(s32[16]{0:T(128)} %param.13) | copy-start | bytes 196
  13.7 5.9 %copy-start.3 = (bf16[16,3968]{1,0:T(8,128)(2,1)S(1)}, bf16[16,3968]{1,0:T(8,128)(2,1)}, u32[]{:S(2)}) copy-start(bf16[16,3968]{1,0:T(8,128)(2,1)} %param.11) | copy-start | bytes 380932
  13.7 54.7 %copy-start.4 = (s32[16,16]{1,0:T(8,128)S(1)}, s32[16,16]{1,0:T(8,128)}, u32[]{:S(2)}) copy-start(s32[16,16]{1,0:T(8,128)} %param.12) | copy-start | bytes 3076
  13.7 54.6 %all-to-all-start = ((bf16[8,2,32,4096]{3,0,2,1:T(8,128)(2,1)}), bf16[8,2,32,4096]{3,0,2,1:T(8,128)(2,1)}, u32[]{:S(2)}, u32[]{:S(2)}) async-start(bf16[8,2,32,4096]{3,0,2,1:T(8,128)(2,1)} %bitcast.44), calls=%async_computation | async-start | bytes 8388608 | tf_op jit(solution)/shard_map/all_to_all | solution.py:41
  75.0 104.0 %copy-start.6 = (s32[64]{0:T(128)S(1)}, s32[64]{0:T(128)}, u32[]{:S(2)}) copy-start(s32[64]{0:T(128)} %param.14) | copy-start | bytes 772
  75.0 108.6 %copy-start.2 = (bf16[8,64,128]{2,1,0:T(8,128)(2,1)S(1)}, bf16[8,64,128]{2,1,0:T(8,128)(2,1)}, u32[]{:S(2)}) copy-start(bf16[8,64,128]{2,1,0:T(8,128)(2,1)} %param.17) | copy-start | bytes 393220
  175.5 7.8 %all-to-all-start.1 = ((bf16[16,32,128]{2,1,0:T(8,128)(2,1)}), bf16[16,32,128]{2,1,0:T(8,128)(2,1)S(1)}, u32[]{:S(2)}, u32[]{:S(2)}) async-start(bf16[16,32,128]{2,1,0:T(8,128)(2,1)} %get-tuple-element.24), calls=%async_computation.1 | async-start | bytes 262144 | tf_op jit(solution)/shard_map/all_to_all | solution.py:52
  178.9 81.0 %all-gather.3.cloned.1.call-start = ((), (), s32[]{:S(2)}) async-start(), calls=%async_computation.2 | async-start | bytes 8912896 | tf_op jit(solution)/shard_map/all_gather | solution.py:62
  183.6 80.2 %copy-start.1 = (f32[8,64,128]{2,1,0:T(8,128)}, f32[8,64,128]{2,1,0:T(8,128)S(1)}, u32[]{:S(2)}) copy-start(f32[8,64,128]{2,1,0:T(8,128)S(1)} %fusion.16) | copy-start | bytes 786436
Sparse Core Ops, SparseCore 0:
  185.0 74.8 all-gather.2
